TPU v7x, 32 devices: a whole 2x2x4 slice. The times are simulated.
32 devices in a mesh: lat: 2 (over core), prop: 16 (over z, y, x).
Axes of the slice: x: 2, y: 2, z: 4, core: 2. Of those that a mesh axis runs over, the one named last changes fastest.
Arguments:
- right_side: float32 [2, 3, 16, 64, 4, 128], P(None, None, None, 'prop', 'lat'), may hold values from -30 to 30
- start_field: float32 [2, 3, 16, 64, 4, 128], P(None, None, None, 'prop', 'lat'), may hold values from -1.75 to 1.75
- region: int32 [64, 4, 128], P('prop', 'lat'), may hold values from 0 to 7
- core_mask: int32 [64, 4, 128], P('prop', 'lat'), may hold values 0 or 1
- intensity: float32 [64, 4, 128], P('prop', 'lat'), may hold values from 0 to 4
- eps_lin: float32 [8], replicated, may hold values from 1 to 12
- eps_loss: float32 [8], replicated, may hold values from 0.1 to 3
- kerr_coef: float32 [8], replicated, may hold values from 0.2 to 1
Outputs:
- new_field: float32 [2, 3, 16, 64, 4, 128], P(None, None, None, 'prop', 'lat')
All inputs are finite; a program needn't handle non-finite values. No bound on the sum of `core_mask` on one device may be relied on, other than what follows from the above.
Results may differ from a plain program's by a relative error of at most 0.00002.
Values sent between devices are 32-bit elements; how exact they have to be, the bound alone decides.
A program may use at most 64 MiB of HBM per device.

v0:
```python
import jax
import jax.numpy as jnp
from jax import lax
from jax.sharding import PartitionSpec as P

wave_sq = 0.25
wave_shift = 0.02
loss_gain = 3.2
tiny = 1e-06


def extended(array, sides, width):
    for axis, dim in sides:
        size, length = (lax.axis_size(axis), array.shape[dim])
        up = [(i, (i + 1) % size) for i in range(size - 1)]
        down = [(j, i) for i, j in up]
        last = lax.slice_in_dim(array, length - width, length, axis=dim)
        first = lax.slice_in_dim(array, 0, width, axis=dim)
        before = lax.ppermute(last, axis, up)
        after = lax.ppermute(first, axis, down)
        array = jnp.concatenate([before, array, after], axis=dim)
    return array


def trimmed(values, direction):
    selector = [slice(None)] * (values.ndim - 3) + [slice(0, -1)] * 3
    if direction is not None:
        selector[values.ndim + direction] = slice(1, None)
    return values[tuple(selector)]


def advance(values, direction):
    return trimmed(values, direction) - trimmed(values, None)


def upper(values, direction):
    selector = [slice(None)] * (values.ndim - 3) + [slice(1, None)] * 3
    if direction is not None:
        selector[values.ndim + direction] = slice(0, -1)
    return values[tuple(selector)]


def retreat(values, direction):
    return upper(values, None) - upper(values, direction)


def curl_twice(padded):
    field_x = padded[:, 0]
    field_y = padded[:, 1]
    field_z = padded[:, 2]
    magnet_x = advance(field_z, -1) - advance(field_y, -3)
    magnet_y = advance(field_x, -3) - advance(field_z, -2)
    magnet_z = advance(field_y, -2) - advance(field_x, -1)
    result_x = retreat(magnet_z, -1) - retreat(magnet_y, -3)
    result_y = retreat(magnet_x, -3) - retreat(magnet_z, -2)
    result_z = retreat(magnet_y, -2) - retreat(magnet_x, -1)
    return jnp.stack([result_x, result_y, result_z], axis=1)


def apply_operator(values, padded, perm_real, perm_imag):
    curled = curl_twice(padded)
    real_part = values[0]
    imag_part = values[1]
    out_real = curled[0] - wave_sq * (perm_real * real_part - perm_imag * imag_part)
    out_imag = curled[1] - wave_sq * (perm_real * imag_part + perm_imag * real_part)
    return jnp.stack([out_real, out_imag])


def ascend(gain_real, gain_imag, forward_value, behind):
    return jnp.stack(
        [
            forward_value[0] + gain_real * behind[0] - gain_imag * behind[1],
            forward_value[1] + gain_real * behind[1] + gain_imag * behind[0],
        ]
    )


def solve_batched(line_data, diag_real, diag_imag):
    depth = line_data.shape[3]
    lines_count = line_data.shape[4] * line_data.shape[5]
    moved = jnp.moveaxis(line_data, 3, 0)
    moved_shape = moved.shape
    rows = moved.reshape((depth, 2, -1))
    repeats = rows.shape[2] // lines_count
    plane_real = diag_real.reshape((depth, lines_count))
    plane_imag = diag_imag.reshape((depth, lines_count))
    unroll_count = min(16, depth)

    def gain_step(carried, element):
        gain_real, gain_imag = carried
        diag_now_real, diag_now_imag = element
        denom_real = diag_now_real - gain_real
        denom_imag = diag_now_imag - gain_imag
        magnitude = denom_real * denom_real + denom_imag * denom_imag
        new_real = denom_real / magnitude
        new_imag = -denom_imag / magnitude
        return ((new_real, new_imag), (new_real, new_imag))

    zero_line = jnp.zeros((lines_count,), jnp.float32)
    unused, (gains_real, gains_imag) = lax.scan(
        gain_step, (zero_line, zero_line), (plane_real, plane_imag), unroll=unroll_count
    )
    wide_real = jnp.tile(gains_real, (1, repeats))
    wide_imag = jnp.tile(gains_imag, (1, repeats))

    def front_step(previous, element):
        gain_real, gain_imag, source = element
        sum_real = source[0] + previous[0]
        sum_imag = source[1] + previous[1]
        updated = jnp.stack(
            [
                gain_real * sum_real - gain_imag * sum_imag,
                gain_real * sum_imag + gain_imag * sum_real,
            ]
        )
        return (updated, updated)

    unused, fronts = lax.scan(
        front_step, jnp.zeros_like(rows[0]), (wide_real, wide_imag, rows), unroll=unroll_count
    )

    def back_step(behind, element):
        gain_real, gain_imag, forward_value = element
        new_value = ascend(gain_real, gain_imag, forward_value, behind)
        return (new_value, new_value)

    unused, values = lax.scan(
        back_step,
        jnp.zeros_like(rows[0]),
        (wide_real, wide_imag, fronts),
        reverse=True,
        unroll=unroll_count,
    )
    return jnp.moveaxis(values.reshape(moved_shape), 0, 3)


def per_device(right_side, start_field, region, core_mask, intensity, eps_lin, eps_loss, kerr_coef):
    levels = jnp.arange(eps_lin.shape[0], dtype=jnp.int32)
    onehot = (region[None] == levels[:, None, None, None]).astype(jnp.float32)
    lin_cell = jnp.sum(onehot * eps_lin[:, None, None, None], axis=0)
    loss_cell = jnp.sum(onehot * eps_loss[:, None, None, None], axis=0)
    kerr_cell = jnp.sum(onehot * kerr_coef[:, None, None, None], axis=0)
    perm_real = lin_cell + core_mask.astype(jnp.float32) * kerr_cell * intensity
    planes = right_side.shape[3]
    total_planes = planes * lax.axis_size("prop")
    diag_real = 2.0 - wave_shift * perm_real
    diag_imag = loss_gain / total_planes * loss_cell

    def operate(values):
        padded = extended(values, (("lat", 4), ("prop", 3)), 1)
        padded = jnp.pad(padded, ((0, 0), (0, 0), (0, 0), (0, 0), (0, 0), (1, 1)))
        return apply_operator(values, padded, perm_real, loss_cell)

    residual = right_side - operate(start_field)
    coeffs = jnp.stack([diag_real, diag_imag])
    line_diag = lax.all_to_all(coeffs, "prop", split_axis=3, concat_axis=1, tiled=True)
    solved = solve_batched(
        lax.all_to_all(residual, "prop", split_axis=5, concat_axis=3, tiled=True),
        line_diag[0],
        line_diag[1],
    )
    precond = lax.all_to_all(solved, "prop", split_axis=3, concat_axis=5, tiled=True)
    image_field = operate(precond)
    cross_sum = jnp.sum(residual * image_field, axis=(0, 1, 3, 4, 5))
    self_sum = jnp.sum(image_field * image_field, axis=(0, 1, 3, 4, 5))
    totals = lax.psum((cross_sum, self_sum), ("lat", "prop"))
    step_size = totals[0] / (totals[1] + tiny)
    return start_field + step_size[None, None, :, None, None, None] * precond


def solution(mesh):
    placed = (
        P(None, None, None, "prop", "lat", None),
        P(None, None, None, "prop", "lat", None),
        P("prop", "lat", None),
        P("prop", "lat", None),
        P("prop", "lat", None),
        P(),
        P(),
        P(),
    )
    return jax.shard_map(
        per_device,
        mesh=mesh,
        in_specs=placed,
        out_specs=P(None, None, None, "prop", "lat", None),
        check_vma=False,
    )
```

profile of v0, /device:TPU:0, one launch (start us, length us, event | category | flops | bytes accessed | tf_op | source)
XLA Modules:
  0.0 232.1 jit_solution(9379006360073458968)
XLA Ops:
  1.2 2.4 %collective-permute-start = (f32[2,3,16,4,1,128]{5,2,4,3,1,0:T(8,128)S(1)}, f32[2,3,16,4,1,128]{5,2,4,3,1,0:T(8,128)S(1)}, u32[]{:S(2)}, u32[]{:S(2)}) collective-permute-start(f32[2,3,16,4,1,128]{5,2,4,3,1,0:T(8,128)S(1)} %get-tuple-element.468), channel_id=1, source_target_pairs={{0,16},{1,17},{2,18},{3,19},{4,20},{5,21},{6,22},{7,23},{8,24},{9,... | collective-permute-start | bytes 589832 | tf_op jit(solution)/shard_map/ppermute | solution.py:19
  6.3 7.7 %all-to-all-start = ((f32[16,1,128]{2,1,0:T(1,128)}), f32[16,1,128]{2,1,0:T(1,128)S(1)}, u32[]{:S(2)}, u32[]{:S(2)}) async-start(f32[16,1,128]{2,1,0:T(1,128)} %reshape.3988), calls=%async_computation | async-start | bytes 16384 | tf_op jit(solution)/shard_map/all_to_all | solution.py:156
  15.4 5.9 %all-to-all-done = f32[16,1,128]{2,1,0:T(1,128)S(1)} async-done(((f32[16,1,128]{2,1,0:T(1,128)}), f32[16,1,128]{2,1,0:T(1,128)S(1)}, u32[]{:S(2)}, u32[]{:S(2)}) %all-to-all-start) | async-done | bytes 8224 | tf_op jit(solution)/shard_map/all_to_all | solution.py:156
  23.6 2.5 %collective-permute-start.2 = (f32[2,3,16,1,4,128]{5,2,4,3,1,0:T(8,128)S(1)}, f32[2,3,16,1,4,128]{5,2,4,3,1,0:T(8,128)S(1)}, u32[]{:S(2)}, u32[]{:S(2)}) collective-permute-start(f32[2,3,16,1,4,128]{5,2,4,3,1,0:T(8,128)S(1)} %get-tuple-element.459), channel_id=1, source_target_pairs={{0,1},{1,2},{2,3},{3,4},{4,5},{5,6},{6,7},{7,8},{8,9},{9,10},{10,1... | collective-permute-start | bytes 589832 | tf_op jit(solution)/shard_map/ppermute | solution.py:19
  29.3 5.3 %collective-permute-done.3 = f32[2,3,16,1,4,128]{5,2,4,3,1,0:T(8,128)S(1)} collective-permute-done((f32[2,3,16,1,4,128]{5,2,4,3,1,0:T(8,128)S(1)}, f32[2,3,16,1,4,128]{5,2,4,3,1,0:T(8,128)S(1)}, u32[]{:S(2)}, u32[]{:S(2)}) %collective-permute-start.3) | collective-permute-done | bytes 196640 | tf_op jit(solution)/shard_map/ppermute | solution.py:20
  39.4 4.9 %reshape.3990 = f32[16,1,6144]{2,1,0:T(1,128)} reshape(f32[128,2,3,4,2,16]{5,4,3,2,1,0:T(2,128)S(1)} %bitcast.1633) | data formatting | bytes 786432
  44.3 4.6 %all-to-all-start.1 = ((f32[16,1,6144]{2,1,0:T(1,128)}), f32[16,1,6144]{2,1,0:T(1,128)S(1)}, u32[]{:S(2)}, u32[]{:S(2)}) async-start(f32[16,1,6144]{2,1,0:T(1,128)} %reshape.3990), calls=%async_computation.1 | async-start | bytes 786432 | tf_op jit(solution)/shard_map/all_to_all | solution.py:158
  49.0 44.4 %while.47 = (s32[]{:T(128)}, f32[16]{0:T(128)S(1)}, f32[16]{0:T(128)S(1)}, f32[4,16,16]{2,1,0:T(8,128)S(1)}, f32[4,16,16]{2,1,0:T(8,128)S(1)}, /*index=5*/f32[4,...) while((s32[]{:T(128)}, f32[16]{0:T(128)S(1)}, ...), condition=%wide.region_4.5_spmd.clone, body=%wide.region_3.4_spmd.clone.sunk | while | flops 2482 | bytes 45483 | solution.py:100
  94.9 2.4 %reduce.1 = f32[16,6144]{1,0:T(8,128)} reduce(f32[16,1,6144]{2,1,0:T(1,128)S(1)} %all-to-all-done.1, f32[]{:T(128)} %broadcast.160), dimensions={1}, to_apply=%all_to_all.40.reduce_sub_computation | reduce | bytes 786436 | tf_op jit(solution)/shard_map/all_to_all | solution.py:158
  97.3 5.3 %reshape.3991 = f32[128,2,3,4,2,16]{5,4,3,2,1,0:T(2,128)S(1)} reshape(f32[16,6144]{1,0:T(8,128)} %reduce.1) | data formatting | bytes 786432
  103.9 2.3 copy.241
  106.2 2.5 %reshape_reshape.6 = f32[4,16,2,768]{1,0,3,2:T(4,128)S(1)} reshape(f32[64,2,3,16,2,8]{0,5,4,3,2,1:T(8,128)} %copy.241) | data formatting | bytes 786432 | tf_op jit(solution)/shard_map/reshape;reshape | solution.py:118
  110.9 9.7 %while.45 = (s32[]{:T(128)}, f32[2,768]{1,0:T(2,128)S(1)}, f32[4,16,2,768]{3,2,1,0:T(2,128)S(1)}, f32[4,16,768]{2,1,0:T(8,128)S(1)}, f32[4,16,2,768]{3,2,1,0:T(2...) while((s32[]{:T(128)}, f32[2,768]{1,0:T(2,128)S(1)}, ...), condition=%wide.region_6.7_spmd, body=%wide.region_5.6_spmd.sunk | while | flops 124432 | bytes 719313 | solution.py:118
  120.8 2.9 %while.46 = (s32[]{:T(128)}, f32[2,768]{1,0:T(2,128)S(1)}, f32[4,16,2,768]{3,2,1,0:T(2,128)S(1)}, f32[4,16,2,768]{3,2,1,0:T(2,128)S(1)}, f32[4,16,768]{2,1,0:T(8...) while((s32[]{:T(128)}, f32[2,768]{1,0:T(2,128)S(1)}, ...), condition=%wide.region_8.9_spmd, body=%wide.region_7.8_spmd.sunk | while | flops 122897 | bytes 713185 | solution.py:127
  124.5 2.8 %copy.243 = f32[4,16,2,768]{1,0,3,2:T(4,128)S(1)} copy(f32[4,16,2,768]{3,2,1,0:T(2,128)} %copy-done.8) | data formatting | bytes 786432 | tf_op jit(solution)/shard_map/while | solution.py:127
  127.3 2.2 reshape_reshape.7
  129.5 2.7 %copy.244 = f32[2,3,16,64,2,8]{2,5,4,1,0,3:T(8,128)S(1)} copy(f32[2,3,16,64,2,8]{3,5,4,2,1,0:T(8,128)} %bitcast.1638) | data formatting | bytes 786432 | tf_op jit(solution)/shard_map/transpose | solution.py:134
  133.3 18.0 %all_to_all.51 = f32[16,1,6144]{2,1,0:T(1,128)S(1)} all-to-all(f32[16,1,6144]{2,1,0:T(1,128)S(1)} %reshape.3992), channel_id=1, replica_groups=mesh['lat'=2,'prop'=16] {'prop'}, dimensions={0} | all-to-all | bytes 786432 | tf_op jit(solution)/shard_map/all_to_all | solution.py:162
  156.6 2.3 copy.279
  161.9 2.7 %copy.247 = f32[2,3,16,4,1,128]{5,2,4,3,1,0:T(8,128)} copy(f32[2,3,16,4,1,128]{2,5,4,3,1,0:T(8,128)} %get-tuple-element.439) | data formatting | bytes 393216 | tf_op jit(solution)/shard_map/slice | solution.py:17
  166.5 2.5 %copy.248 = f32[2,3,16,4,1,128]{5,2,4,3,1,0:T(8,128)} copy(f32[2,3,16,4,1,128]{2,5,4,3,1,0:T(8,128)} %get-tuple-element.440) | data formatting | bytes 393216 | tf_op jit(solution)/shard_map/slice | solution.py:18
  174.3 3.2 %collective-permute-start.6 = (f32[2,3,16,1,4,128]{5,2,4,3,1,0:T(8,128)}, f32[2,3,16,1,4,128]{5,2,4,3,1,0:T(8,128)}, u32[]{:S(2)}, u32[]{:S(2)}) collective-permute-start(f32[2,3,16,1,4,128]{5,2,4,3,1,0:T(8,128)} %get-tuple-element.454), channel_id=1, source_target_pairs={{0,1},{1,2},{2,3},{3,4},{4,5},{5,6},{6,7},{7,8},{8,9},{9,10},{10,1... | collective-permute-start | bytes 589832 | tf_op jit(solution)/shard_map/ppermute | solution.py:19
  181.5 6.4 %collective-permute-done.7 = f32[2,3,16,1,4,128]{5,2,4,3,1,0:T(8,128)} collective-permute-done((f32[2,3,16,1,4,128]{5,2,4,3,1,0:T(8,128)}, f32[2,3,16,1,4,128]{5,2,4,3,1,0:T(8,128)}, u32[]{:S(2)}, u32[]{:S(2)}) %collective-permute-start.7) | collective-permute-done | bytes 196640 | tf_op jit(solution)/shard_map/ppermute | solution.py:20
  192.0 39.0 %all-reduce.2 = (f32[16]{0:T(128)S(1)}, f32[16]{0:T(128)S(1)}) all-reduce(f32[16]{0:T(128)S(1)} %get-tuple-element.262, f32[16]{0:T(128)S(1)} %get-tuple-element.261), channel_id=1, replica_groups=mesh['lat'=2,'prop'=16] {'lat','prop'}, use_global_device_ids=true, to_apply=%region_10.11 | all-reduce | flops 32 | bytes 256 | tf_op jit(solution)/shard_map/psum | solution.py:166
  (335 shorter events, 103.0 us)
Async XLA Ops:
  0.0 23.5 %copy-start.2 = (f32[2,3,16,4,2,128]{5,4,3,2,1,0:T(2,128)S(1)}, f32[2,3,16,4,2,128]{5,4,3,2,1,0:T(2,128)}, u32[]{:S(2)}) copy-start(f32[2,3,16,4,2,128]{5,4,3,2,1,0:T(2,128)} %param.15) | copy-start | bytes 1179652
  1.2 22.2 %collective-permute-start = (f32[2,3,16,4,1,128]{5,2,4,3,1,0:T(8,128)S(1)}, f32[2,3,16,4,1,128]{5,2,4,3,1,0:T(8,128)S(1)}, u32[]{:S(2)}, u32[]{:S(2)}) collective-permute-start(f32[2,3,16,4,1,128]{5,2,4,3,1,0:T(8,128)S(1)} %get-tuple-element.468), channel_id=1, source_target_pairs={{0,16},{1,17},{2,18},{3,19},{4,20},{5,21},{6,22},{7,23},{8,24},{9,... | collective-permute-start | bytes 589832 | tf_op jit(solution)/shard_map/ppermute | solution.py:19
  6.3 14.9 %all-to-all-start = ((f32[16,1,128]{2,1,0:T(1,128)}), f32[16,1,128]{2,1,0:T(1,128)S(1)}, u32[]{:S(2)}, u32[]{:S(2)}) async-start(f32[16,1,128]{2,1,0:T(1,128)} %reshape.3988), calls=%async_computation | async-start | bytes 16384 | tf_op jit(solution)/shard_map/all_to_all | solution.py:156
  14.0 9.5 %collective-permute-start.1 = (f32[2,3,16,4,1,128]{5,2,4,3,1,0:T(8,128)S(1)}, f32[2,3,16,4,1,128]{5,2,4,3,1,0:T(8,128)S(1)}, u32[]{:S(2)}, u32[]{:S(2)}) collective-permute-start(f32[2,3,16,4,1,128]{5,2,4,3,1,0:T(8,128)S(1)} %get-tuple-element.467), channel_id=1, source_target_pairs={{16,0},{17,1},{18,2},{19,3},{20,4},{21,5},{22,6},{23,7},{24,8},{25... | collective-permute-start | bytes 589832 | tf_op jit(solution)/shard_map/ppermute | solution.py:20
  23.6 5.7 %collective-permute-start.2 = (f32[2,3,16,1,4,128]{5,2,4,3,1,0:T(8,128)S(1)}, f32[2,3,16,1,4,128]{5,2,4,3,1,0:T(8,128)S(1)}, u32[]{:S(2)}, u32[]{:S(2)}) collective-permute-start(f32[2,3,16,1,4,128]{5,2,4,3,1,0:T(8,128)S(1)} %get-tuple-element.459), channel_id=1, source_target_pairs={{0,1},{1,2},{2,3},{3,4},{4,5},{5,6},{6,7},{7,8},{8,9},{9,10},{10,1... | collective-permute-start | bytes 589832 | tf_op jit(solution)/shard_map/ppermute | solution.py:19
  26.1 8.5 %collective-permute-start.3 = (f32[2,3,16,1,4,128]{5,2,4,3,1,0:T(8,128)S(1)}, f32[2,3,16,1,4,128]{5,2,4,3,1,0:T(8,128)S(1)}, u32[]{:S(2)}, u32[]{:S(2)}) collective-permute-start(f32[2,3,16,1,4,128]{5,2,4,3,1,0:T(8,128)S(1)} %get-tuple-element.460), channel_id=1, source_target_pairs={{1,0},{2,1},{3,2},{4,3},{5,4},{6,5},{7,6},{8,7},{9,8},{10,9},{11,1... | collective-permute-start | bytes 589832 | tf_op jit(solution)/shard_map/ppermute | solution.py:20
  35.9 1.2 copy-start.9
  36.3 0.7 copy-start.6
  39.4 9.6 %copy-start.13 = (f32[4,16,16]{2,1,0:T(8,128)S(1)}, f32[4,16,16]{2,1,0:T(8,128)}, u32[]{:S(2)}) copy-start(f32[4,16,16]{2,1,0:T(8,128)} %custom-call.5) | copy-start | bytes 12292
  39.4 9.6 %copy-start.14 = (f32[4,16,16]{2,1,0:T(8,128)S(1)}, f32[4,16,16]{2,1,0:T(8,128)}, u32[]{:S(2)}) copy-start(f32[4,16,16]{2,1,0:T(8,128)} %custom-call.6) | copy-start | bytes 12292
  44.3 50.6 %all-to-all-start.1 = ((f32[16,1,6144]{2,1,0:T(1,128)}), f32[16,1,6144]{2,1,0:T(1,128)S(1)}, u32[]{:S(2)}, u32[]{:S(2)}) async-start(f32[16,1,6144]{2,1,0:T(1,128)} %reshape.3990), calls=%async_computation.1 | async-start | bytes 786432 | tf_op jit(solution)/shard_map/all_to_all | solution.py:158
  123.7 0.7 copy-start.8
  153.9 2.7 %copy-start = (f32[64,2,3,2,8,16]{5,4,3,2,1,0:T(8,128)}, f32[64,2,3,2,8,16]{5,4,3,2,1,0:T(8,128)S(1)}, u32[]{:S(2)}) copy-start(f32[64,2,3,2,8,16]{5,4,3,2,1,0:T(8,128)S(1)} %reshape.3993) | copy-start | bytes 1179652
  161.9 8.5 %copy-start.1 = (f32[2,3,16,64,2,8]{2,5,4,3,1,0:T(8,128)S(1)}, f32[2,3,16,64,2,8]{2,5,4,3,1,0:T(8,128)}, u32[]{:S(2)}) copy-start(f32[2,3,16,64,2,8]{2,5,4,3,1,0:T(8,128)} %copy.245) | copy-start | bytes 1179652
  164.6 6.2 %collective-permute-start.4 = (f32[2,3,16,4,1,128]{5,2,4,3,1,0:T(8,128)}, f32[2,3,16,4,1,128]{5,2,4,3,1,0:T(8,128)}, u32[]{:S(2)}, u32[]{:S(2)}) collective-permute-start(f32[2,3,16,4,1,128]{5,2,4,3,1,0:T(8,128)} %copy.247), channel_id=1, source_target_pairs={{0,16},{1,17},{2,18},{3,19},{4,20},{5,21},{6,22},{7,23},{8,24},{9,... | collective-permute-start | bytes 589832 | tf_op jit(solution)/shard_map/ppermute | solution.py:19
  169.1 3.5 %collective-permute-start.5 = (f32[2,3,16,4,1,128]{5,2,4,3,1,0:T(8,128)}, f32[2,3,16,4,1,128]{5,2,4,3,1,0:T(8,128)S(1)}, u32[]{:S(2)}, u32[]{:S(2)}) collective-permute-start(f32[2,3,16,4,1,128]{5,2,4,3,1,0:T(8,128)} %copy.248), channel_id=1, source_target_pairs={{16,0},{17,1},{18,2},{19,3},{20,4},{21,5},{22,6},{23,7},{24,8},{25... | collective-permute-start | bytes 589832 | tf_op jit(solution)/shard_map/ppermute | solution.py:20
  172.6 6.5 %copy-start.12 = (f32[2,3,16,4,1,128]{5,2,4,3,1,0:T(8,128)}, f32[2,3,16,4,1,128]{5,2,4,3,1,0:T(8,128)S(1)}, u32[]{:S(2)}) copy-start(f32[2,3,16,4,1,128]{5,2,4,3,1,0:T(8,128)S(1)} %collective-permute-done.5) | copy-start | bytes 589828
  174.3 7.2 %collective-permute-start.6 = (f32[2,3,16,1,4,128]{5,2,4,3,1,0:T(8,128)}, f32[2,3,16,1,4,128]{5,2,4,3,1,0:T(8,128)}, u32[]{:S(2)}, u32[]{:S(2)}) collective-permute-start(f32[2,3,16,1,4,128]{5,2,4,3,1,0:T(8,128)} %get-tuple-element.454), channel_id=1, source_target_pairs={{0,1},{1,2},{2,3},{3,4},{4,5},{5,6},{6,7},{7,8},{8,9},{9,10},{10,1... | collective-permute-start | bytes 589832 | tf_op jit(solution)/shard_map/ppermute | solution.py:19
  177.4 10.5 %collective-permute-start.7 = (f32[2,3,16,1,4,128]{5,2,4,3,1,0:T(8,128)}, f32[2,3,16,1,4,128]{5,2,4,3,1,0:T(8,128)}, u32[]{:S(2)}, u32[]{:S(2)}) collective-permute-start(f32[2,3,16,1,4,128]{5,2,4,3,1,0:T(8,128)} %get-tuple-element.455), channel_id=1, source_target_pairs={{1,0},{2,1},{3,2},{4,3},{5,4},{6,5},{7,6},{8,7},{9,8},{10,9},{11,1... | collective-permute-start | bytes 589832 | tf_op jit(solution)/shard_map/ppermute | solution.py:20
  190.4 0.9 copy-start.11
  190.4 1.0 copy-start.5
  190.4 1.1 copy-start.7
  190.5 1.3 copy-start.10
  190.5 40.5 %copy-start.3 = (f32[2,3,16,4,2,128]{5,4,3,2,1,0:T(2,128)S(1)}, f32[2,3,16,4,2,128]{5,4,3,2,1,0:T(2,128)}, u32[]{:S(2)}) copy-start(f32[2,3,16,4,2,128]{5,4,3,2,1,0:T(2,128)} %param.15) | copy-start | bytes 1179652
  (1 other events, 0.7 us)
where the time goes:
time: 236 us; the launch traced here: 232 us
  other arithmetic  67.8 us (29%)
  local copies, waits for them, and re-layouts  57.5 us (24%)
  blocking collectives  57 us (24%)
  starting transfers between devices  27.5 us (12%)
  waiting for transfers between devices  20.7 us (9%)
    psum x1, blocking collectives, per_device(): totals = lax.psum((cross_sum, self_sum), ('lat', 'prop'))  39 us
    sub x28, other arithmetic, gain_step(): denom_imag = diag_now_imag - gain_imag  21.5 us
    sub x28, other arithmetic, gain_step(): denom_real = diag_now_real - gain_real  19.4 us
    all_to_all x1, blocking collectives, per_device(): lax.all_to_all(solved, 'prop', split_axis=3, concat_axis=5, tiled=True)  18 us
    unnamed x39, local copies, waits for them, and re-layouts  17.8 us
    ppermute x4, waiting for transfers between devices, extended(): after = lax.ppermute(first, axis, down)  13.6 us
    ppermute x4, starting transfers between devices, extended(): before = lax.ppermute(last, axis, up)  10.1 us
    all_to_all x1, starting transfers between devices, per_device(): lax.all_to_all(coeffs, 'prop', split_axis=3, concat_axis=1, tiled=True)  7.68 us
  transfers between devices with their start and end apart: 10, of which 6 were waited for; matrix products, arithmetic and copies ran while one was open for 25% of the time, Pallas kernels for 0%

commit v1 on v0

--- a/solution.py
+++ b/solution.py
@@ -7,6 +7,28 @@
 wave_shift = 0.02
 loss_gain = 3.2
 tiny = 1e-06
+
+
+def split_up(x, dim, count):
+    before, after = (x.shape[:dim], x.shape[dim + 1 :])
+    return jnp.moveaxis(x.reshape(*before, count, -1, *after), dim, 0)
+
+
+def in_order(tiles, dim):
+    shape = list(tiles.shape[1:])
+    shape[dim] *= tiles.shape[0]
+    return jnp.moveaxis(tiles, 0, dim).reshape(shape)
+
+
+def exchange_in_pairs(value, axis, split_dim, concat_dim):
+    devices, place = (lax.axis_size(axis), lax.axis_index(axis))
+    blocks = split_up(value, split_dim, devices)
+    outs = [blocks[place]]
+    for lap in range(1, devices):
+        sent = blocks[place ^ lap]
+        outs.append(lax.ppermute(sent, axis, [(i, i ^ lap) for i in range(devices)]))
+    blocks = jnp.stack(outs)[place ^ jnp.arange(devices)]
+    return in_order(blocks, concat_dim)
 
 
 def extended(array, sides, width):
@@ -159,7 +181,7 @@
         line_diag[0],
         line_diag[1],
     )
-    precond = lax.all_to_all(solved, "prop", split_axis=3, concat_axis=5, tiled=True)
+    precond = exchange_in_pairs(solved, "prop", 3, 5)
     image_field = operate(precond)
     cross_sum = jnp.sum(residual * image_field, axis=(0, 1, 3, 4, 5))
     self_sum = jnp.sum(image_field * image_field, axis=(0, 1, 3, 4, 5))

time: 236 us -> 304 us (1.29)
  starting transfers between devices: 27.5 us -> 77.2 us
  waiting for transfers between devices: 20.7 us -> 38.2 us
  local copies, waits for them, and re-layouts: 57.5 us -> 67.6 us
  blocking collectives: 57 us -> 48.5 us
    ppermute x0 -> x15, starting transfers between devices: none -> 48.3 us  [exchange_in_pairs(): lax.ppermute(sent, axis, [(i, i ^ lap) for i in range(devices)])]
    all_to_all x1 -> x0, blocking collectives: 18 us -> none  [per_device(): lax.all_to_all(solved, 'prop', split_axis=3, concat_axis=5, tiled=True)]
    ppermute x0 -> x15, waiting for transfers between devices: none -> 14.8 us  [exchange_in_pairs(): lax.ppermute(sent, axis, [(i, i ^ lap) for i in range(devices)])]
    psum x1, blocking collectives: 39 us -> 48.5 us  [per_device(): totals = lax.psum((cross_sum, self_sum), ('lat', 'prop'))]
    unnamed x39 -> x50, local copies, waits for them, and re-layouts: 17.8 us -> 27.1 us
    all_to_all x3 -> x0, local copies, waits for them, and re-layouts: 5.51 us -> none  [per_device(): lax.all_to_all(solved, 'prop', split_axis=3, concat_axis=5, tiled=True)]
  transfers between devices with their start and end apart: 10 -> 25, of which waited for: 6 -> 14; matrix products, arithmetic and copies ran while one was open for 25% -> 23% of each run, Pallas kernels for 0% -> 0%
where the time goes in v1:
time: 304 us; the launch traced here: 300 us
  starting transfers between devices  77.2 us (25%)
  local copies, waits for them, and re-layouts  67.6 us (22%)
  other arithmetic  67.2 us (22%)
  blocking collectives  48.5 us (16%)
  waiting for transfers between devices  38.2 us (13%)
    psum x1, blocking collectives, per_device(): totals = lax.psum((cross_sum, self_sum), ('lat', 'prop'))  48.5 us
    ppermute x15, starting transfers between devices, exchange_in_pairs(): lax.ppermute(sent, axis, [(i, i ^ lap) for i in range(devices)])  48.3 us
    unnamed x50, local copies, waits for them, and re-layouts  27.1 us
    sub x28, other arithmetic, gain_step(): denom_imag = diag_now_imag - gain_imag  21.6 us
    sub x28, other arithmetic, gain_step(): denom_real = diag_now_real - gain_real  19.6 us
    ppermute x4, waiting for transfers between devices, extended(): after = lax.ppermute(first, axis, down)  14.8 us
    ppermute x15, waiting for transfers between devices, exchange_in_pairs(): lax.ppermute(sent, axis, [(i, i ^ lap) for i in range(devices)])  14.8 us
    ppermute x4, starting transfers between devices, extended(): before = lax.ppermute(last, axis, up)  12.3 us
  transfers between devices with their start and end apart: 25, of which 14 were waited for; matrix products, arithmetic and copies ran while one was open for 23% of the time, Pallas kernels for 0%

profile of v1, /device:TPU:0, one launch (start us, length us, event | category | flops | bytes accessed | tf_op | source)
XLA Modules:
  0.0 300.2 jit_solution(15742929061336354933)
XLA Ops:
  7.6 7.7 %all-to-all-start = ((f32[16,1,128]{2,1,0:T(1,128)}), f32[16,1,128]{2,1,0:T(1,128)S(1)}, u32[]{:S(2)}, u32[]{:S(2)}) async-start(f32[16,1,128]{2,1,0:T(1,128)} %reshape.4051), calls=%async_computation | async-start | bytes 16384 | tf_op jit(solution)/shard_map/all_to_all | solution.py:178
  15.9 6.6 %all-to-all-done = f32[16,1,128]{2,1,0:T(1,128)S(1)} async-done(((f32[16,1,128]{2,1,0:T(1,128)}), f32[16,1,128]{2,1,0:T(1,128)S(1)}, u32[]{:S(2)}, u32[]{:S(2)}) %all-to-all-start) | async-done | bytes 8224 | tf_op jit(solution)/shard_map/all_to_all | solution.py:178
  25.0 2.5 collective-permute-start.2
  31.5 6.1 %collective-permute-done.3 = f32[2,3,16,1,4,128]{5,2,4,3,1,0:T(8,128)S(1)} collective-permute-done((f32[2,3,16,1,4,128]{5,2,4,3,1,0:T(8,128)S(1)}, f32[2,3,16,1,4,128]{5,2,4,3,1,0:T(8,128)S(1)}, u32[]{:S(2)}, u32[]{:S(2)}) %collective-permute-start.3) | collective-permute-done | bytes 196640 | tf_op jit(solution)/shard_map/ppermute | solution.py:42
  42.4 4.9 %reshape.4053 = f32[16,1,6144]{2,1,0:T(1,128)} reshape(f32[128,2,3,4,2,16]{5,4,3,2,1,0:T(2,128)S(1)} %bitcast.1690) | data formatting | bytes 786432
  47.3 3.8 %all-to-all-start.1 = ((f32[16,1,6144]{2,1,0:T(1,128)}), f32[16,1,6144]{2,1,0:T(1,128)S(1)}, u32[]{:S(2)}, u32[]{:S(2)}) async-start(f32[16,1,6144]{2,1,0:T(1,128)} %reshape.4053), calls=%async_computation.1 | async-start | bytes 786432 | tf_op jit(solution)/shard_map/all_to_all | solution.py:180
  51.2 44.6 %while.47 = (s32[]{:T(128)}, f32[16]{0:T(128)S(1)}, f32[16]{0:T(128)S(1)}, f32[4,16,16]{2,1,0:T(8,128)S(1)}, f32[4,16,16]{2,1,0:T(8,128)S(1)}, /*index=5*/f32[4,...) while((s32[]{:T(128)}, f32[16]{0:T(128)S(1)}, ...), condition=%wide.region_4.5_spmd.clone, body=%wide.region_3.4_spmd.clone.sunk | while | flops 2482 | bytes 45483 | solution.py:122
  99.8 5.3 %reshape.4054 = f32[128,2,3,4,2,16]{5,4,3,2,1,0:T(2,128)S(1)} reshape(f32[16,6144]{1,0:T(8,128)} %reduce.1) | data formatting | bytes 786432
  108.7 2.5 reshape_reshape.6
  113.4 9.7 %while.45 = (s32[]{:T(128)}, f32[2,768]{1,0:T(2,128)S(1)}, f32[4,16,2,768]{3,2,1,0:T(2,128)S(1)}, f32[4,16,768]{2,1,0:T(8,128)S(1)}, f32[4,16,2,768]{3,2,1,0:T(2...) while((s32[]{:T(128)}, f32[2,768]{1,0:T(2,128)S(1)}, ...), condition=%wide.region_6.7_spmd, body=%wide.region_5.6_spmd.sunk | while | flops 124432 | bytes 719313 | solution.py:140
  123.3 2.9 while.46
  127.0 2.8 copy.279
  142.5 2.7 collective-permute-start.9
  152.1 4.2 %collective-permute-start.12 = (f32[2,3,16,4,2,8]{2,5,4,3,1,0:T(8,128)S(1)}, f32[2,3,16,4,2,8]{2,5,4,3,1,0:T(8,128)S(1)}, u32[]{:S(2)}, u32[]{:S(2)}) collective-permute-start(f32[2,3,16,4,2,8]{2,5,4,3,1,0:T(8,128)S(1)} %get-tuple-element.453), channel_id=1, source_target_pairs={{0,9},{1,8},{2,11},{3,10},{4,13},{5,12},{6,15},{7,14},{8,1},{9,0},... | collective-permute-start | bytes 73736 | tf_op jit(solution)/shard_map/ppermute | solution.py:29
  161.7 3.2 %collective-permute-done.9 = f32[2,3,16,4,2,8]{2,5,4,3,1,0:T(8,128)S(1)} collective-permute-done((f32[2,3,16,4,2,8]{2,5,4,3,1,0:T(8,128)S(1)}, f32[2,3,16,4,2,8]{2,5,4,3,1,0:T(8,128)S(1)}, u32[]{:S(2)}, u32[]{:S(2)}) %collective-permute-start.9) | collective-permute-done | bytes 24608 | tf_op jit(solution)/shard_map/ppermute | solution.py:29
  171.4 17.5 %collective-permute-start.16 = (f32[2,3,16,4,2,8]{2,5,4,3,1,0:T(8,128)S(1)}, f32[2,3,16,4,2,8]{2,5,4,3,1,0:T(8,128)S(1)}, u32[]{:S(2)}, u32[]{:S(2)}) collective-permute-start(f32[2,3,16,4,2,8]{2,5,4,3,1,0:T(8,128)S(1)} %get-tuple-element.449), channel_id=1, source_target_pairs={{0,13},{1,12},{2,15},{3,14},{4,9},{5,8},{6,11},{7,10},{8,5},{9,4},... | collective-permute-start | bytes 73736 | tf_op jit(solution)/shard_map/ppermute | solution.py:29
  189.6 5.4 %collective-permute-done.12 = f32[2,3,16,4,2,8]{2,5,4,3,1,0:T(8,128)S(1)} collective-permute-done((f32[2,3,16,4,2,8]{2,5,4,3,1,0:T(8,128)S(1)}, f32[2,3,16,4,2,8]{2,5,4,3,1,0:T(8,128)S(1)}, u32[]{:S(2)}, u32[]{:S(2)}) %collective-permute-start.12) | collective-permute-done | bytes 24608 | tf_op jit(solution)/shard_map/ppermute | solution.py:29
  196.7 8.0 %collective-permute-start.18 = (f32[2,3,16,4,2,8]{2,5,4,3,1,0:T(8,128)S(1)}, f32[2,3,16,4,2,8]{2,5,4,3,1,0:T(8,128)S(1)}, u32[]{:S(2)}, u32[]{:S(2)}) collective-permute-start(f32[2,3,16,4,2,8]{2,5,4,3,1,0:T(8,128)S(1)} %get-tuple-element.447), channel_id=1, source_target_pairs={{0,15},{1,14},{2,13},{3,12},{4,11},{5,10},{6,9},{7,8},{8,7},{9,6},... | collective-permute-start | bytes 73736 | tf_op jit(solution)/shard_map/ppermute | solution.py:29
  209.1 2.8 gather_fusion
  218.1 2.5 copy.282
  222.6 2.5 copy.283
  230.4 5.4 %collective-permute-start.21 = (f32[2,3,16,1,4,128]{5,2,4,3,1,0:T(8,128)}, f32[2,3,16,1,4,128]{5,2,4,3,1,0:T(8,128)}, u32[]{:S(2)}, u32[]{:S(2)}) collective-permute-start(f32[2,3,16,1,4,128]{5,2,4,3,1,0:T(8,128)} %get-tuple-element.475), channel_id=1, source_target_pairs={{0,1},{1,2},{2,3},{3,4},{4,5},{5,6},{6,7},{7,8},{8,9},{9,10},{10,1... | collective-permute-start | bytes 589832 | tf_op jit(solution)/shard_map/ppermute | solution.py:41
  239.8 6.8 %collective-permute-done.22 = f32[2,3,16,1,4,128]{5,2,4,3,1,0:T(8,128)} collective-permute-done((f32[2,3,16,1,4,128]{5,2,4,3,1,0:T(8,128)}, f32[2,3,16,1,4,128]{5,2,4,3,1,0:T(8,128)}, u32[]{:S(2)}, u32[]{:S(2)}) %collective-permute-start.22) | collective-permute-done | bytes 196640 | tf_op jit(solution)/shard_map/ppermute | solution.py:42
  250.6 48.5 %all-reduce.2 = (f32[16]{0:T(128)S(1)}, f32[16]{0:T(128)S(1)}) all-reduce(f32[16]{0:T(128)S(1)} %get-tuple-element.268, f32[16]{0:T(128)S(1)} %get-tuple-element.267), channel_id=1, replica_groups=mesh['lat'=2,'prop'=16] {'lat','prop'}, use_global_device_ids=true, to_apply=%region_10.11 | all-reduce | flops 32 | bytes 256 | tf_op jit(solution)/shard_map/psum | solution.py:188
  (378 shorter events, 147.1 us)
Async XLA Ops:
  1.2 23.6 %collective-permute-start = (f32[2,3,16,4,1,128]{5,2,4,3,1,0:T(8,128)S(1)}, f32[2,3,16,4,1,128]{5,2,4,3,1,0:T(8,128)S(1)}, u32[]{:S(2)}, u32[]{:S(2)}) collective-permute-start(f32[2,3,16,4,1,128]{5,2,4,3,1,0:T(8,128)S(1)} %get-tuple-element.489), channel_id=1, source_target_pairs={{0,16},{1,17},{2,18},{3,19},{4,20},{5,21},{6,22},{7,23},{8,24},{9,... | collective-permute-start | bytes 589832 | tf_op jit(solution)/shard_map/ppermute | solution.py:41
  3.6 21.3 %collective-permute-start.1 = (f32[2,3,16,4,1,128]{5,2,4,3,1,0:T(8,128)S(1)}, f32[2,3,16,4,1,128]{5,2,4,3,1,0:T(8,128)S(1)}, u32[]{:S(2)}, u32[]{:S(2)}) collective-permute-start(f32[2,3,16,4,1,128]{5,2,4,3,1,0:T(8,128)S(1)} %get-tuple-element.488), channel_id=1, source_target_pairs={{16,0},{17,1},{18,2},{19,3},{20,4},{21,5},{22,6},{23,7},{24,8},{25... | collective-permute-start | bytes 589832 | tf_op jit(solution)/shard_map/ppermute | solution.py:42
  7.6 14.9 %all-to-all-start = ((f32[16,1,128]{2,1,0:T(1,128)}), f32[16,1,128]{2,1,0:T(1,128)S(1)}, u32[]{:S(2)}, u32[]{:S(2)}) async-start(f32[16,1,128]{2,1,0:T(1,128)} %reshape.4051), calls=%async_computation | async-start | bytes 16384 | tf_op jit(solution)/shard_map/all_to_all | solution.py:178
  25.0 6.5 %collective-permute-start.2 = (f32[2,3,16,1,4,128]{5,2,4,3,1,0:T(8,128)S(1)}, f32[2,3,16,1,4,128]{5,2,4,3,1,0:T(8,128)S(1)}, u32[]{:S(2)}, u32[]{:S(2)}) collective-permute-start(f32[2,3,16,1,4,128]{5,2,4,3,1,0:T(8,128)S(1)} %get-tuple-element.480), channel_id=1, source_target_pairs={{0,1},{1,2},{2,3},{3,4},{4,5},{5,6},{6,7},{7,8},{8,9},{9,10},{10,1... | collective-permute-start | bytes 589832 | tf_op jit(solution)/shard_map/ppermute | solution.py:41
  27.5 10.1 %collective-permute-start.3 = (f32[2,3,16,1,4,128]{5,2,4,3,1,0:T(8,128)S(1)}, f32[2,3,16,1,4,128]{5,2,4,3,1,0:T(8,128)S(1)}, u32[]{:S(2)}, u32[]{:S(2)}) collective-permute-start(f32[2,3,16,1,4,128]{5,2,4,3,1,0:T(8,128)S(1)} %get-tuple-element.481), channel_id=1, source_target_pairs={{1,0},{2,1},{3,2},{4,3},{5,4},{6,5},{7,6},{8,7},{9,8},{10,9},{11,1... | collective-permute-start | bytes 589832 | tf_op jit(solution)/shard_map/ppermute | solution.py:42
  47.3 50.0 %all-to-all-start.1 = ((f32[16,1,6144]{2,1,0:T(1,128)}), f32[16,1,6144]{2,1,0:T(1,128)S(1)}, u32[]{:S(2)}, u32[]{:S(2)}) async-start(f32[16,1,6144]{2,1,0:T(1,128)} %reshape.4053), calls=%async_computation.1 | async-start | bytes 786432 | tf_op jit(solution)/shard_map/all_to_all | solution.py:180
  134.9 7.6 %collective-permute-start.4 = (f32[2,3,16,4,2,8]{2,5,4,3,1,0:T(8,128)S(1)}, f32[2,3,16,4,2,8]{2,5,4,3,1,0:T(8,128)S(1)}, u32[]{:S(2)}, u32[]{:S(2)}) collective-permute-start(f32[2,3,16,4,2,8]{2,5,4,3,1,0:T(8,128)S(1)} %get-tuple-element.461), channel_id=1, source_target_pairs={{0,1},{1,0},{2,3},{3,2},{4,5},{5,4},{6,7},{7,6},{8,9},{9,8},{10,11... | collective-permute-start | bytes 73736 | tf_op jit(solution)/shard_map/ppermute | solution.py:29
  137.6 9.7 %collective-permute-start.5 = (f32[2,3,16,4,2,8]{2,5,4,3,1,0:T(8,128)S(1)}, f32[2,3,16,4,2,8]{2,5,4,3,1,0:T(8,128)S(1)}, u32[]{:S(2)}, u32[]{:S(2)}) collective-permute-start(f32[2,3,16,4,2,8]{2,5,4,3,1,0:T(8,128)S(1)} %get-tuple-element.460), channel_id=1, source_target_pairs={{0,2},{1,3},{2,0},{3,1},{4,6},{5,7},{6,4},{7,5},{8,10},{9,11},{10,... | collective-permute-start | bytes 73736 | tf_op jit(solution)/shard_map/ppermute | solution.py:29
  139.0 10.0 %collective-permute-start.6 = (f32[2,3,16,4,2,8]{2,5,4,3,1,0:T(8,128)S(1)}, f32[2,3,16,4,2,8]{2,5,4,3,1,0:T(8,128)S(1)}, u32[]{:S(2)}, u32[]{:S(2)}) collective-permute-start(f32[2,3,16,4,2,8]{2,5,4,3,1,0:T(8,128)S(1)} %get-tuple-element.459), channel_id=1, source_target_pairs={{0,3},{1,2},{2,1},{3,0},{4,7},{5,6},{6,5},{7,4},{8,11},{9,10},{10,... | collective-permute-start | bytes 73736 | tf_op jit(solution)/shard_map/ppermute | solution.py:29
  139.2 13.0 %collective-permute-start.7 = (f32[2,3,16,4,2,8]{2,5,4,3,1,0:T(8,128)S(1)}, f32[2,3,16,4,2,8]{2,5,4,3,1,0:T(8,128)S(1)}, u32[]{:S(2)}, u32[]{:S(2)}) collective-permute-start(f32[2,3,16,4,2,8]{2,5,4,3,1,0:T(8,128)S(1)} %get-tuple-element.458), channel_id=1, source_target_pairs={{0,4},{1,5},{2,6},{3,7},{4,0},{5,1},{6,2},{7,3},{8,12},{9,13},{10,... | collective-permute-start | bytes 73736 | tf_op jit(solution)/shard_map/ppermute | solution.py:29
  141.1 17.9 %collective-permute-start.8 = (f32[2,3,16,4,2,8]{2,5,4,3,1,0:T(8,128)S(1)}, f32[2,3,16,4,2,8]{2,5,4,3,1,0:T(8,128)S(1)}, u32[]{:S(2)}, u32[]{:S(2)}) collective-permute-start(f32[2,3,16,4,2,8]{2,5,4,3,1,0:T(8,128)S(1)} %get-tuple-element.457), channel_id=1, source_target_pairs={{0,5},{1,4},{2,7},{3,6},{4,1},{5,0},{6,3},{7,2},{8,13},{9,12},{10,... | collective-permute-start | bytes 73736 | tf_op jit(solution)/shard_map/ppermute | solution.py:29
  142.5 22.3 %collective-permute-start.9 = (f32[2,3,16,4,2,8]{2,5,4,3,1,0:T(8,128)S(1)}, f32[2,3,16,4,2,8]{2,5,4,3,1,0:T(8,128)S(1)}, u32[]{:S(2)}, u32[]{:S(2)}) collective-permute-start(f32[2,3,16,4,2,8]{2,5,4,3,1,0:T(8,128)S(1)} %get-tuple-element.456), channel_id=1, source_target_pairs={{0,6},{1,7},{2,4},{3,5},{4,2},{5,3},{6,0},{7,1},{8,14},{9,15},{10,... | collective-permute-start | bytes 73736 | tf_op jit(solution)/shard_map/ppermute | solution.py:29
  147.3 21.5 %collective-permute-start.10 = (f32[2,3,16,4,2,8]{2,5,4,3,1,0:T(8,128)S(1)}, f32[2,3,16,4,2,8]{2,5,4,3,1,0:T(8,128)S(1)}, u32[]{:S(2)}, u32[]{:S(2)}) collective-permute-start(f32[2,3,16,4,2,8]{2,5,4,3,1,0:T(8,128)S(1)} %get-tuple-element.455), channel_id=1, source_target_pairs={{0,7},{1,6},{2,5},{3,4},{4,3},{5,2},{6,1},{7,0},{8,15},{9,14},{10,... | collective-permute-start | bytes 73736 | tf_op jit(solution)/shard_map/ppermute | solution.py:29
  149.0 22.4 %collective-permute-start.11 = (f32[2,3,16,4,2,8]{2,5,4,3,1,0:T(8,128)S(1)}, f32[2,3,16,4,2,8]{2,5,4,3,1,0:T(8,128)S(1)}, u32[]{:S(2)}, u32[]{:S(2)}) collective-permute-start(f32[2,3,16,4,2,8]{2,5,4,3,1,0:T(8,128)S(1)} %get-tuple-element.454), channel_id=1, source_target_pairs={{0,8},{1,9},{2,10},{3,11},{4,12},{5,13},{6,14},{7,15},{8,0},{9,1},... | collective-permute-start | bytes 73736 | tf_op jit(solution)/shard_map/ppermute | solution.py:29
  152.1 42.9 %collective-permute-start.12 = (f32[2,3,16,4,2,8]{2,5,4,3,1,0:T(8,128)S(1)}, f32[2,3,16,4,2,8]{2,5,4,3,1,0:T(8,128)S(1)}, u32[]{:S(2)}, u32[]{:S(2)}) collective-permute-start(f32[2,3,16,4,2,8]{2,5,4,3,1,0:T(8,128)S(1)} %get-tuple-element.453), channel_id=1, source_target_pairs={{0,9},{1,8},{2,11},{3,10},{4,13},{5,12},{6,15},{7,14},{8,1},{9,0},... | collective-permute-start | bytes 73736 | tf_op jit(solution)/shard_map/ppermute | solution.py:29
  158.9 37.8 %collective-permute-start.13 = (f32[2,3,16,4,2,8]{2,5,4,3,1,0:T(8,128)S(1)}, f32[2,3,16,4,2,8]{2,5,4,3,1,0:T(8,128)S(1)}, u32[]{:S(2)}, u32[]{:S(2)}) collective-permute-start(f32[2,3,16,4,2,8]{2,5,4,3,1,0:T(8,128)S(1)} %get-tuple-element.452), channel_id=1, source_target_pairs={{0,10},{1,11},{2,8},{3,9},{4,14},{5,15},{6,12},{7,13},{8,2},{9,3},... | collective-permute-start | bytes 73736 | tf_op jit(solution)/shard_map/ppermute | solution.py:29
  164.8 40.6 %collective-permute-start.14 = (f32[2,3,16,4,2,8]{2,5,4,3,1,0:T(8,128)S(1)}, f32[2,3,16,4,2,8]{2,5,4,3,1,0:T(8,128)S(1)}, u32[]{:S(2)}, u32[]{:S(2)}) collective-permute-start(f32[2,3,16,4,2,8]{2,5,4,3,1,0:T(8,128)S(1)} %get-tuple-element.451), channel_id=1, source_target_pairs={{0,11},{1,10},{2,9},{3,8},{4,15},{5,14},{6,13},{7,12},{8,3},{9,2},... | collective-permute-start | bytes 73736 | tf_op jit(solution)/shard_map/ppermute | solution.py:29
  168.8 37.3 %collective-permute-start.15 = (f32[2,3,16,4,2,8]{2,5,4,3,1,0:T(8,128)S(1)}, f32[2,3,16,4,2,8]{2,5,4,3,1,0:T(8,128)S(1)}, u32[]{:S(2)}, u32[]{:S(2)}) collective-permute-start(f32[2,3,16,4,2,8]{2,5,4,3,1,0:T(8,128)S(1)} %get-tuple-element.450), channel_id=1, source_target_pairs={{0,12},{1,13},{2,14},{3,15},{4,8},{5,9},{6,10},{7,11},{8,4},{9,5},... | collective-permute-start | bytes 73736 | tf_op jit(solution)/shard_map/ppermute | solution.py:29
  171.4 35.4 %collective-permute-start.16 = (f32[2,3,16,4,2,8]{2,5,4,3,1,0:T(8,128)S(1)}, f32[2,3,16,4,2,8]{2,5,4,3,1,0:T(8,128)S(1)}, u32[]{:S(2)}, u32[]{:S(2)}) collective-permute-start(f32[2,3,16,4,2,8]{2,5,4,3,1,0:T(8,128)S(1)} %get-tuple-element.449), channel_id=1, source_target_pairs={{0,13},{1,12},{2,15},{3,14},{4,9},{5,8},{6,11},{7,10},{8,5},{9,4},... | collective-permute-start | bytes 73736 | tf_op jit(solution)/shard_map/ppermute | solution.py:29
  195.0 12.5 %collective-permute-start.17 = (f32[2,3,16,4,2,8]{2,5,4,3,1,0:T(8,128)S(1)}, f32[2,3,16,4,2,8]{2,5,4,3,1,0:T(8,128)S(1)}, u32[]{:S(2)}, u32[]{:S(2)}) collective-permute-start(f32[2,3,16,4,2,8]{2,5,4,3,1,0:T(8,128)S(1)} %get-tuple-element.448), channel_id=1, source_target_pairs={{0,14},{1,15},{2,12},{3,13},{4,10},{5,11},{6,8},{7,9},{8,6},{9,7},... | collective-permute-start | bytes 73736 | tf_op jit(solution)/shard_map/ppermute | solution.py:29
  196.7 11.7 %collective-permute-start.18 = (f32[2,3,16,4,2,8]{2,5,4,3,1,0:T(8,128)S(1)}, f32[2,3,16,4,2,8]{2,5,4,3,1,0:T(8,128)S(1)}, u32[]{:S(2)}, u32[]{:S(2)}) collective-permute-start(f32[2,3,16,4,2,8]{2,5,4,3,1,0:T(8,128)S(1)} %get-tuple-element.447), channel_id=1, source_target_pairs={{0,15},{1,14},{2,13},{3,12},{4,11},{5,10},{6,9},{7,8},{8,7},{9,6},... | collective-permute-start | bytes 73736 | tf_op jit(solution)/shard_map/ppermute | solution.py:29
  220.6 6.2 %collective-permute-start.19 = (f32[2,3,16,4,1,128]{5,2,4,3,1,0:T(8,128)}, f32[2,3,16,4,1,128]{5,2,4,3,1,0:T(8,128)}, u32[]{:S(2)}, u32[]{:S(2)}) collective-permute-start(f32[2,3,16,4,1,128]{5,2,4,3,1,0:T(8,128)} %copy.282), channel_id=1, source_target_pairs={{0,16},{1,17},{2,18},{3,19},{4,20},{5,21},{6,22},{7,23},{8,24},{9,... | collective-permute-start | bytes 589832 | tf_op jit(solution)/shard_map/ppermute | solution.py:41
  230.4 9.5 %collective-permute-start.21 = (f32[2,3,16,1,4,128]{5,2,4,3,1,0:T(8,128)}, f32[2,3,16,1,4,128]{5,2,4,3,1,0:T(8,128)}, u32[]{:S(2)}, u32[]{:S(2)}) collective-permute-start(f32[2,3,16,1,4,128]{5,2,4,3,1,0:T(8,128)} %get-tuple-element.475), channel_id=1, source_target_pairs={{0,1},{1,2},{2,3},{3,4},{4,5},{5,6},{6,7},{7,8},{8,9},{9,10},{10,1... | collective-permute-start | bytes 589832 | tf_op jit(solution)/shard_map/ppermute | solution.py:41
  235.7 10.9 %collective-permute-start.22 = (f32[2,3,16,1,4,128]{5,2,4,3,1,0:T(8,128)}, f32[2,3,16,1,4,128]{5,2,4,3,1,0:T(8,128)}, u32[]{:S(2)}, u32[]{:S(2)}) collective-permute-start(f32[2,3,16,1,4,128]{5,2,4,3,1,0:T(8,128)} %get-tuple-element.476), channel_id=1, source_target_pairs={{1,0},{2,1},{3,2},{4,3},{5,4},{6,5},{7,6},{8,7},{9,8},{10,9},{11,1... | collective-permute-start | bytes 589832 | tf_op jit(solution)/shard_map/ppermute | solution.py:42
  (15 other events, 113.7 us)
